TPU v7x, 256 devices: a whole 4x4x8 slice. The times are simulated.
256 devices in a mesh: pop: 32 (over x_lo, z, core), tp: 8 (over x_hi, y).
Axes of the slice: x: 4 (x_hi: 2, x_lo: 2; x = x_hi * 2 + x_lo), y: 4, z: 8, core: 2. Of those that a mesh axis runs over, the one named last changes fastest.
Arguments:
- hidden: bfloat16 [2048, 5120], P('pop', 'tp'), may hold values from -24 to 24
- norm_gain: float32 [5120], P('tp'), may hold values from 0.25 to 1.75
- right_factors: bfloat16 [5120, 128], P('tp'), may hold values from -0.078125 to 0.078125
- left_factors: bfloat16 [77824, 128], P(('pop', 'tp')), may hold values from -4 to 4
- targets: int32 [2048], replicated, may hold values from 0 to 77823
- master: float32 [77824, 5120], P(('pop', 'tp')), may hold values from -0.2934839 to 0.2934839
Outputs:
- member_loglik: float32 [64], replicated
- new_master: float32 [77824, 5120], P(('pop', 'tp'))
All inputs are finite; a program needn't handle non-finite values.
Results may differ from a plain program's by a relative error of at most 0.0026.
The roundings to bfloat16 on the way count: a program that leaves them out, or rounds other values in their place, can miss the bound.
Values may be sent and summed in bfloat16 or wider, within the bound.
A program may use at most 128 MiB of HBM per device.

v0:
```python
import jax
import jax.numpy as jnp
from jax import lax
from jax.sharding import PartitionSpec as P

D = 5120
RANK = 4
SEQ = 32
NORM_EPS = 1e-06
SIGMA_NOISE = 0.25
LEARN_RATE = 0.5


def contract(left, right):
    return lax.dot_general(
        left, right, (((1,), (1,)), ((), ())), preferred_element_type=jnp.float32
    )


def body(hidden, norm_gain, right_factors, left_factors, targets, master):
    tok_rows = hidden.shape[0]
    half_rows = tok_rows // 2
    fact_cols = right_factors.shape[1]
    voc_rows = master.shape[0]
    pop_index = lax.axis_index("pop")
    values = hidden.astype(jnp.float32)
    squares = lax.psum(jnp.sum(values * values, axis=1), "tp")
    row_scale = lax.rsqrt(squares / D + NORM_EPS)
    normed = (values * row_scale[:, None] * norm_gain[None, :]).astype(jnp.bfloat16)
    pair_cols = lax.dynamic_slice_in_dim(right_factors, pop_index * RANK, RANK, 1)
    partial_proj = jnp.dot(normed, pair_cols, preferred_element_type=jnp.float32)
    projection = lax.psum(partial_proj, "tp")
    member_sign = jnp.where(jnp.arange(tok_rows) < half_rows, SIGMA_NOISE, -SIGMA_NOISE).astype(
        jnp.float32
    )
    scaled = projection * member_sign[:, None]
    own_block = (lax.iota(jnp.int32, fact_cols) // RANK == pop_index).astype(jnp.float32)
    lowrank = (jnp.tile(scaled, (1, fact_cols // RANK)) * own_block[None, :]).astype(jnp.bfloat16)
    head = master.astype(jnp.bfloat16)
    full_rows, full_right = (
        lax.all_gather(normed, "tp", axis=1, tiled=True),
        lax.all_gather(right_factors, "tp", axis=0, tiled=True),
    )
    joined_rows = jnp.concatenate([full_rows, lowrank], axis=1)
    piece = lax.all_gather(joined_rows, "pop", axis=0, tiled=True)
    logits = contract(piece[:, :D], head) + contract(piece[:, D:], left_factors)
    offset = (pop_index * lax.axis_size("tp") + lax.axis_index("tp")) * voc_rows
    row_max = jnp.max(logits, axis=1)
    column_ids = lax.iota(jnp.int32, voc_rows)
    target_logit = jnp.sum(
        jnp.where(offset + column_ids[None, :] == targets[:, None], logits, 0.0), axis=1
    )
    all_max = lax.pmax(row_max, ("pop", "tp"))
    row_sum = jnp.sum(jnp.exp(logits - all_max[:, None]), axis=1)
    all_sum, all_target = lax.psum((row_sum, target_logit), ("pop", "tp"))
    logprob = all_target - all_max - jnp.log(all_sum)
    member_loglik = jnp.mean(logprob.reshape(-1, SEQ), axis=1)
    fitness = member_loglik[0::2] - member_loglik[1::2]
    weight_cols = jnp.repeat(fitness, RANK)
    scaled_left = (left_factors.astype(jnp.float32) * weight_cols[None, :]).astype(jnp.bfloat16)
    update = contract(scaled_left, full_right)
    new_master = master + LEARN_RATE * update
    return (member_loglik, new_master)


def solution(mesh):
    in_specs = (
        P("pop", "tp"),
        P("tp"),
        P("tp", None),
        P(("pop", "tp"), None),
        P(),
        P(("pop", "tp"), None),
    )
    out_specs = (P(), P(("pop", "tp"), None))
    return jax.shard_map(body, mesh=mesh, in_specs=in_specs, out_specs=out_specs, check_vma=False)
```

profile of v0, /device:TPU:1, one launch (start us, length us, event | category | flops | bytes accessed | tf_op | source)
XLA Modules:
  0.0 395.4 jit_solution(13763955117740881840)
XLA Ops:
  7.3 1.0 fusion.11
  8.3 21.5 %psum.28 = f32[64]{0:T(128)S(1)} all-reduce(f32[64]{0:T(128)S(1)} %fusion.11), channel_id=1, replica_groups=mesh['pop'=32,'tp'=8] {'tp'}, use_global_device_ids=true, to_apply=%region_1.0 | all-reduce | flops 64 | bytes 512 | tf_op jit(solution)/shard_map/psum | solution.py:27
  29.8 1.0 fusion.13
  30.8 29.9 %all_gather.9 = bf16[64,5120]{1,0:T(8,128)(2,1)S(1)} all-gather(bf16[64,640]{1,0:T(8,128)(2,1)S(1)} %fusion.13), channel_id=1, replica_groups=mesh['pop'=32,'tp'=8] {'tp'}, dimensions={1}, use_global_device_ids=true | all-gather | bytes 737280 | tf_op jit(solution)/shard_map/all_gather | solution.py:41
  60.7 1.2 fusion.14
  61.8 15.7 %psum.29 = f32[64,4]{0,1:T(4,128)S(1)} all-reduce(f32[64,4]{0,1:T(4,128)S(1)} %fusion.14), channel_id=1, replica_groups=mesh['pop'=32,'tp'=8] {'tp'}, use_global_device_ids=true, to_apply=%region_2.0 | all-reduce | flops 256 | bytes 2048 | tf_op jit(solution)/shard_map/psum | solution.py:32
  77.6 0.1 multiply_convert_fusion.2
  77.7 0.1 copy.9
  77.8 0.9 pad_maximum_fusion
  78.7 0.0 all-gather.5.cloned.1.call-start
  78.7 0.7 all-gather.5.cloned.1.call-update
  79.5 135.6 %all-gather.3.cloned.1.call-done = bf16[2048,5248]{1,0:T(8,128)(2,1)} async-done(((bf16[64,5248]{1,0:T(8,128)(2,1)}), bf16[2048,5248]{1,0:T(8,128)(2,1)}) %all-gather.3.cloned.1.call-update) | async-done | bytes 21495824 | tf_op jit(solution)/shard_map/all_gather | solution.py:45
  215.0 1.5 fusion.9
  216.6 12.6 %fusion.18 = (f32[2048]{0:T(1024)S(1)}, f32[2048,304]{0,1:T(8,128)S(1)}) fusion(f32[2048,304]{0,1:T(8,128)S(1)} %fusion.9, f32[304,5120]{1,0:T(8,128)} %param.11, bf16[2048,5248]{1,0:T(8,128)(2,1)} %all-gather.3.cloned.1.call-done), kind=kOutput, calls=%fused_computation.33 | convolution fusion | flops 6378141696 | bytes 32186368 | tf_op jit(solution)/shard_map/dot_general | solution.py:15
  229.2 78.5 %pmax.7 = f32[2048]{0:T(1024)S(1)} all-reduce(f32[2048]{0:T(1024)S(1)} %get-tuple-element.6), channel_id=1, replica_groups=mesh['pop'=32,'tp'=8] {'pop','tp'}, use_global_device_ids=true, to_apply=%region_6.7 | all-reduce | flops 2048 | bytes 16384 | tf_op jit(solution)/shard_map/pmax | solution.py:53
  307.8 0.6 select_reduce_fusion
  308.4 72.7 %all-reduce = (f32[2048]{0:T(1024)S(1)}, f32[2048]{0:T(1024)S(1)}) all-reduce(f32[2048]{0:T(1024)S(1)} %get-tuple-element.3, f32[2048]{0:T(1024)S(1)} %get-tuple-element.2), channel_id=1, replica_groups=mesh['pop'=32,'tp'=8] {'pop','tp'}, use_global_device_ids=true, to_apply=%region_8.9 | all-reduce | flops 4096 | bytes 32768 | tf_op jit(solution)/shard_map/psum | solution.py:55
  381.1 0.1 reshape.41
  381.1 0.1 reduce_sum.39
  381.3 0.1 slice.14
  381.4 0.1 slice.15
  381.5 0.1 broadcast_in_dim.25
  381.6 0.1 mul.72
  381.7 6.8 %fusion.2 = f32[304,5120]{1,0:T(8,128)} fusion(f32[304,5120]{1,0:T(8,128)} %param.11, bf16[5120,128]{1,0:T(8,128)(2,1)} %all-gather.5.cloned.1.call-done, bf16[304,128]{1,0:T(8,128)(2,1)S(1)} %copy-done, f32[128]{0:T(128)S(1)} %mul.72), kind=kOutput, calls=%fused_computation.3 | convolution fusion | flops 401688576 | bytes 13840896 | tf_op jit(solution)/shard_map/dot_general | solution.py:15
  (18 shorter events, 0.2 us)
Async XLA Ops:
  7.2 207.9 %copy-start = (bf16[304,128]{1,0:T(8,128)(2,1)S(1)}, bf16[304,128]{1,0:T(8,128)(2,1)}, u32[]{:S(2)}) copy-start(bf16[304,128]{1,0:T(8,128)(2,1)} %param.9) | copy-start | bytes 233476
  7.2 207.9 %all-gather.3.cloned.1.call-start = ((), (), s32[]{:S(2)}) async-start(), calls=%async_computation | async-start | bytes 22167552 | tf_op jit(solution)/shard_map/all_gather | solution.py:45
  78.7 303.1 %all-gather.5.cloned.1.call-start = ((), (), s32[]{:S(2)}) async-start(), calls=%async_computation.1 | async-start | bytes 1474560 | tf_op jit(solution)/shard_map/all_gather | solution.py:42
  216.6 91.2 %copy-start.1 = (s32[2048]{0:T(1024)S(1)}, s32[2048]{0:T(1024)}, u32[]{:S(2)}) copy-start(s32[2048]{0:T(1024)} %param.10) | copy-start | bytes 24580
  381.3 7.3 %copy-start.2 = (f32[64]{0:T(128)}, f32[64]{0:T(128)S(1)}, u32[]{:S(2)}) copy-start(f32[64]{0:T(128)S(1)} %broadcast_multiply_fusion.1) | copy-start | bytes 772
Sparse Core Ops, SparseCore 0:
  78.8 136.1 all-gather.2
  217.6 52.0 all-gather.4
where the time goes:
time: 396 us; the launch traced here: 395 us
  blocking collectives  218 us (55%)
  waiting for transfers between devices  136 us (34%)
  matrix products  22.2 us (6%)
  between operations  14.2 us (4%)
    all_gather x1, waiting for transfers between devices, body(): piece = lax.all_gather(joined_rows, 'pop', axis=0, tiled=True)  136 us
    pmax x1, blocking collectives, body(): all_max = lax.pmax(row_max, ('pop', 'tp'))  78.5 us
    psum x1, blocking collectives, body(): all_sum, all_target = lax.psum((row_sum, target_logit), ('pop', 'tp'))  72.7 us
    all_gather x1, blocking collectives, body(): lax.all_gather(normed, 'tp', axis=1, tiled=True)  29.9 us
    psum x1, blocking collectives, body(): squares = lax.psum(jnp.sum(values * values, axis=1), 'tp')  21.5 us
    dot_general x3, matrix products, contract(): lax.dot_general(left, right, (((1,), (1,)), ((), ())), preferred_element_...  21 us
    psum x1, blocking collectives, body(): projection = lax.psum(partial_proj, 'tp')  15.7 us
  transfers between devices with their start and end apart: 2, of which 1 were waited for; matrix products, arithmetic and copies ran while one was open for 4% of the time, Pallas kernels for 0%

commit v1 on v0

--- a/solution.py
+++ b/solution.py
@@ -52,7 +52,11 @@
     )
     all_max = lax.pmax(row_max, ("pop", "tp"))
     row_sum = jnp.sum(jnp.exp(logits - all_max[:, None]), axis=1)
-    all_sum, all_target = lax.psum((row_sum, target_logit), ("pop", "tp"))
+
+    def touch_region(local_array):
+        return lax.psum(lax.psum(local_array, "pop"), "tp")
+
+    all_sum, all_target = touch_region((row_sum, target_logit))
     logprob = all_target - all_max - jnp.log(all_sum)
     member_loglik = jnp.mean(logprob.reshape(-1, SEQ), axis=1)
     fitness = member_loglik[0::2] - member_loglik[1::2]

time: 396 us -> 465 us (1.17)
  the two profiles are of different devices: /device:TPU:1 before, /device:TPU:6 now
where the time goes in v1:
time: 465 us
  blocking collectives  299 us (64%)
  waiting for transfers between devices  125 us (27%)
  matrix products  22.2 us (5%)
  between operations  14.2 us (3%)
    psum x2, blocking collectives, touch_region(): return lax.psum(lax.psum(local_array, 'pop'), 'tp')  145 us
    all_gather x1, waiting for transfers between devices, body(): piece = lax.all_gather(joined_rows, 'pop', axis=0, tiled=True)  124 us
    pmax x1, blocking collectives, body(): all_max = lax.pmax(row_max, ('pop', 'tp'))  77 us
    all_gather x1, blocking collectives, body(): lax.all_gather(normed, 'tp', axis=1, tiled=True)  35.2 us
    psum x1, blocking collectives, body(): squares = lax.psum(jnp.sum(values * values, axis=1), 'tp')  22.8 us
    dot_general x3, matrix products, contract(): lax.dot_general(left, right, (((1,), (1,)), ((), ())), preferred_element_...  21 us
    psum x1, blocking collectives, body(): projection = lax.psum(partial_proj, 'tp')  19.3 us
  transfers between devices with their start and end apart: 2, of which 1 were waited for; matrix products, arithmetic and copies ran while one was open for 3% of the time, Pallas kernels for 0%

profile of v1, /device:TPU:6, one launch (start us, length us, event | category | flops | bytes accessed | tf_op | source)
XLA Modules:
  0.0 464.8 jit_solution(401056864205948864)
XLA Ops:
  7.3 1.0 fusion.11
  8.3 22.8 %psum.42 = f32[64]{0:T(128)S(1)} all-reduce(f32[64]{0:T(128)S(1)} %fusion.11), channel_id=1, replica_groups=mesh['pop'=32,'tp'=8] {'tp'}, use_global_device_ids=true, to_apply=%region_1.0 | all-reduce | flops 64 | bytes 512 | tf_op jit(solution)/shard_map/psum | solution.py:27
  31.1 1.0 fusion.13
  32.1 35.2 %all_gather.9 = bf16[64,5120]{1,0:T(8,128)(2,1)S(1)} all-gather(bf16[64,640]{1,0:T(8,128)(2,1)S(1)} %fusion.13), channel_id=1, replica_groups=mesh['pop'=32,'tp'=8] {'tp'}, dimensions={1}, use_global_device_ids=true | all-gather | bytes 737280 | tf_op jit(solution)/shard_map/all_gather | solution.py:41
  67.3 1.2 fusion.14
  68.5 19.3 %psum.43 = f32[64,4]{0,1:T(4,128)S(1)} all-reduce(f32[64,4]{0,1:T(4,128)S(1)} %fusion.14), channel_id=1, replica_groups=mesh['pop'=32,'tp'=8] {'tp'}, use_global_device_ids=true, to_apply=%region_2.0 | all-reduce | flops 256 | bytes 2048 | tf_op jit(solution)/shard_map/psum | solution.py:32
  87.9 0.1 multiply_convert_fusion.2
  88.0 0.1 copy.9
  88.0 0.9 pad_maximum_fusion
  89.0 0.7 all-gather.5.cloned.1.call-update
  89.7 123.9 %all-gather.3.cloned.1.call-done = bf16[2048,5248]{1,0:T(8,128)(2,1)} async-done(((bf16[64,5248]{1,0:T(8,128)(2,1)}), bf16[2048,5248]{1,0:T(8,128)(2,1)}) %all-gather.3.cloned.1.call-update) | async-done | bytes 21495824 | tf_op jit(solution)/shard_map/all_gather | solution.py:45
  213.6 1.5 fusion.9
  215.2 12.7 %fusion.18 = (f32[2048]{0:T(1024)S(1)}, f32[2048,304]{0,1:T(8,128)S(1)}) fusion(f32[2048,304]{0,1:T(8,128)S(1)} %fusion.9, f32[304,5120]{1,0:T(8,128)} %param.11, bf16[2048,5248]{1,0:T(8,128)(2,1)} %all-gather.3.cloned.1.call-done), kind=kOutput, calls=%fused_computation.33 | convolution fusion | flops 6378141696 | bytes 32186368 | tf_op jit(solution)/shard_map/dot_general | solution.py:15
  227.8 77.0 %pmax.7 = f32[2048]{0:T(1024)S(1)} all-reduce(f32[2048]{0:T(1024)S(1)} %get-tuple-element.8), channel_id=1, replica_groups=mesh['pop'=32,'tp'=8] {'pop','tp'}, use_global_device_ids=true, to_apply=%region_7.8 | all-reduce | flops 2048 | bytes 16384 | tf_op jit(solution)/shard_map/pmax | solution.py:53
  304.8 0.6 select_reduce_fusion
  305.4 105.8 %all-reduce = (f32[2048]{0:T(1024)S(1)}, f32[2048]{0:T(1024)S(1)}) all-reduce(f32[2048]{0:T(1024)S(1)} %get-tuple-element.3, f32[2048]{0:T(1024)S(1)} %get-tuple-element.2), channel_id=1, replica_groups=mesh['pop'=32,'tp'=8] {'pop'}, use_global_device_ids=true, to_apply=%region_9.10 | all-reduce | flops 4096 | bytes 32768 | tf_op jit(solution)/shard_map/psum | solution.py:57
  411.2 39.3 %all-reduce.1 = (f32[2048]{0:T(1024)S(1)}, f32[2048]{0:T(1024)S(1)}) all-reduce(f32[2048]{0:T(1024)S(1)} %get-tuple-element.4, f32[2048]{0:T(1024)S(1)} %get-tuple-element.5), channel_id=1, replica_groups=mesh['pop'=32,'tp'=8] {'tp'}, use_global_device_ids=true, to_apply=%region_10.11 | all-reduce | flops 4096 | bytes 32768 | tf_op jit(solution)/shard_map/psum | solution.py:57
  450.5 0.1 reshape.41
  450.5 0.1 reduce_sum.39
  450.7 0.1 slice.14
  450.8 0.1 slice.15
  450.9 0.1 broadcast_in_dim.25
  451.0 0.1 mul.72
  451.2 6.8 %fusion.2 = f32[304,5120]{1,0:T(8,128)} fusion(f32[304,5120]{1,0:T(8,128)} %param.11, bf16[5120,128]{1,0:T(8,128)(2,1)} %all-gather.5.cloned.1.call-done, bf16[304,128]{1,0:T(8,128)(2,1)S(1)} %copy-done, f32[128]{0:T(128)S(1)} %mul.72), kind=kOutput, calls=%fused_computation.3 | convolution fusion | flops 401688576 | bytes 13840896 | tf_op jit(solution)/shard_map/dot_general | solution.py:15
  (19 shorter events, 0.2 us)
Async XLA Ops:
  7.2 206.5 %copy-start = (bf16[304,128]{1,0:T(8,128)(2,1)S(1)}, bf16[304,128]{1,0:T(8,128)(2,1)}, u32[]{:S(2)}) copy-start(bf16[304,128]{1,0:T(8,128)(2,1)} %param.9) | copy-start | bytes 233476
  7.2 206.4 %all-gather.3.cloned.1.call-start = ((), (), s32[]{:S(2)}) async-start(), calls=%async_computation | async-start | bytes 22167552 | tf_op jit(solution)/shard_map/all_gather | solution.py:45
  89.0 362.2 %all-gather.5.cloned.1.call-start = ((), (), s32[]{:S(2)}) async-start(), calls=%async_computation.1 | async-start | bytes 1474560 | tf_op jit(solution)/shard_map/all_gather | solution.py:42
  215.1 89.6 %copy-start.1 = (s32[2048]{0:T(1024)S(1)}, s32[2048]{0:T(1024)}, u32[]{:S(2)}) copy-start(s32[2048]{0:T(1024)} %param.10) | copy-start | bytes 24580
  450.7 7.3 %copy-start.2 = (f32[64]{0:T(128)}, f32[64]{0:T(128)S(1)}, u32[]{:S(2)}) copy-start(f32[64]{0:T(128)S(1)} %broadcast_multiply_fusion.1) | copy-start | bytes 772
Sparse Core Ops, SparseCore 0:
  89.1 124.4 all-gather.2
  216.2 51.9 all-gather.4
